TPU v7x, 32 devices: a whole 2x2x4 slice. The times are simulated.
32 devices in a mesh: clus: 8 (over z, core), node: 4 (over y, x).
Axes of the slice: x: 2, y: 2, z: 4, core: 2. Of those that a mesh axis runs over, the one named last changes fastest.
Arguments:
- node_feats: bfloat16 [8, 512, 1024], P('clus', 'node'), may hold values from -6 to 6
- cotangent: bfloat16 [8, 512, 1024], P('clus', 'node'), may hold values from -6 to 6
- w_query: bfloat16 [1024, 1024], replicated, may hold values from -0.1875 to 0.1875
- w_key: bfloat16 [1024, 1024], replicated, may hold values from -0.1875 to 0.1875
- w_value: bfloat16 [1024, 1024], replicated, may hold values from -0.1875 to 0.1875
- w_out: bfloat16 [1024, 1024], replicated, may hold values from -0.1875 to 0.1875
- eigvec: bfloat16 [8, 64, 512], P('clus'), may hold values from -3.5 to 3.5
- eig_weight: float32 [16, 64], P('node'), may hold values from 0.1 to 1
- block_mask: int32 [8, 16, 4, 4], P('clus', 'node'), may hold values from 0 to 1, as said below
Outputs:
- grad_nodes: bfloat16 [8, 512, 1024], P('clus', 'node')
- grad_eigvec: float32 [8, 64, 512], P('clus', None, 'node')
- grad_weight: float32 [16, 64], P('node')
- grad_proj: float32 [4, 1024, 1024], P(None, 'clus', 'node')
Inputs may be any that keep to these rules, and one draw needn't show every extreme that they name: `block_mask`: each entry is 0 or 1; every diagonal tile is 1; the share of present tiles differs between clusters and heads.
All inputs are finite; a program needn't handle non-finite values.
Results may differ from a plain program's by a relative error of at most 0.012.
The roundings to bfloat16 on the way count: a program that leaves them out, or rounds other values in their place, can miss the bound.
Values may be sent and summed in bfloat16 or wider, within the bound.
No kernel may reach another device: no remote copies, remote signals or barrier semaphores. Data moves between devices by JAX's collectives and lax.ppermute only.
A program may use at most 128 MiB of HBM per device.

v0:
```python
import jax
import jax.numpy as jnp
from jax import lax
from jax.sharding import PartitionSpec as P


def body(node_feats, cotangent, w_query, w_key, w_value, w_out, eigvec, eig_weight, block_mask):
    node_rows = node_feats[0]
    grads_in = cotangent[0]
    query = jnp.dot(node_rows, w_query, preferred_element_type=jnp.float32).astype(jnp.bfloat16)
    keys_local = jnp.dot(node_rows, w_key, preferred_element_type=jnp.float32).astype(jnp.bfloat16)
    values_local = jnp.dot(node_rows, w_value, preferred_element_type=jnp.float32).astype(
        jnp.bfloat16
    )
    d_att = jnp.dot(grads_in, w_out, preferred_element_type=jnp.float32).astype(jnp.bfloat16)
    head_data = lax.all_to_all(
        jnp.stack([query, keys_local, values_local, d_att]),
        "node",
        split_axis=2,
        concat_axis=1,
        tiled=True,
    )
    node_count = head_data.shape[1]
    head_width = head_data.shape[2]
    heads_dev = eig_weight.shape[0]
    head_size = head_width // heads_dev
    by_head = head_data.reshape(4, node_count, heads_dev, head_size)
    query_heads = by_head[0]
    keys_heads = by_head[1]
    values_heads = by_head[2]
    dout_heads = by_head[3]
    eig_all = eigvec[0]
    eig_float = eig_all.astype(jnp.float32)
    weighted = (eig_weight[:, :, None] * eig_float[None]).astype(jnp.bfloat16)
    tile_mask = block_mask[0]
    tile_count = tile_mask.shape[2]
    tile_size = node_count // tile_count
    block_rows = min(512, node_count)
    block_count = node_count // block_rows
    score_scale = head_size ** (-0.5)

    def one_block(totals, block_index):
        key_grad, value_grad, eig_right, weight_grad = totals
        offset = block_index * block_rows
        query_block = lax.dynamic_slice_in_dim(query_heads, offset, block_rows, 0)
        dout_block = lax.dynamic_slice_in_dim(dout_heads, offset, block_rows, 0)
        eig_block = lax.dynamic_slice_in_dim(eig_all, offset, block_rows, 1)
        eig_bias = jnp.einsum(
            "ki,hkj->hij", eig_block, weighted, preferred_element_type=jnp.float32
        )
        scores = (
            jnp.einsum("ihd,jhd->hij", query_block, keys_heads, preferred_element_type=jnp.float32)
            * score_scale
            + eig_bias
        )
        tile_rows = lax.dynamic_slice_in_dim(
            tile_mask, offset // tile_size, block_rows // tile_size, 1
        )
        present = jnp.broadcast_to(
            tile_rows[:, :, None, :, None] > 0,
            (heads_dev, block_rows // tile_size, tile_size, tile_count, tile_size),
        )
        present = present.reshape(heads_dev, block_rows, node_count)
        masked = jnp.where(present, scores, -jnp.inf)
        row_max = jnp.max(masked, axis=2, keepdims=True)
        raised = jnp.exp(masked - row_max)
        attn_prob = raised / jnp.sum(raised, axis=2, keepdims=True)
        prob_half = attn_prob.astype(jnp.bfloat16)
        out_block = jnp.einsum(
            "hij,jhd->ihd", prob_half, values_heads, preferred_element_type=jnp.float32
        ).astype(jnp.bfloat16)
        dprob = jnp.einsum(
            "ihd,jhd->hij", dout_block, values_heads, preferred_element_type=jnp.float32
        )
        row_delta = jnp.sum(attn_prob * dprob, axis=2, keepdims=True)
        dscore = (attn_prob * (dprob - row_delta)).astype(jnp.bfloat16)
        query_grad = (
            jnp.einsum("hij,jhd->ihd", dscore, keys_heads, preferred_element_type=jnp.float32)
            * score_scale
        ).astype(jnp.bfloat16)
        key_grad = key_grad + jnp.einsum(
            "hij,ihd->jhd", dscore, query_block, preferred_element_type=jnp.float32
        )
        value_grad = value_grad + jnp.einsum(
            "hij,ihd->jhd", prob_half, dout_block, preferred_element_type=jnp.float32
        )
        eig_left = jnp.einsum("hij,kj->hki", dscore, eig_all, preferred_element_type=jnp.float32)
        weight_grad = weight_grad + jnp.sum(eig_left * eig_block.astype(jnp.float32)[None], axis=2)
        eig_right = eig_right + jnp.einsum(
            "hij,ki->hkj", dscore, eig_block, preferred_element_type=jnp.float32
        )
        left_term = jnp.sum(eig_weight[:, :, None] * eig_left, axis=0)
        return ((key_grad, value_grad, eig_right, weight_grad), (out_block, query_grad, left_term))

    initial = (
        jnp.zeros((node_count, heads_dev, head_size), jnp.float32),
        jnp.zeros((node_count, heads_dev, head_size), jnp.float32),
        jnp.zeros((heads_dev, eig_all.shape[0], node_count), jnp.float32),
        jnp.zeros(eig_weight.shape, jnp.float32),
    )
    totals, blocks = lax.scan(one_block, initial, jnp.arange(block_count))
    output_heads = blocks[0].reshape(node_count, head_width)
    query_grad_heads = blocks[1].reshape(node_count, head_width)
    key_grad_heads = (totals[0] * score_scale).astype(jnp.bfloat16).reshape(node_count, head_width)
    value_grad_heads = totals[1].astype(jnp.bfloat16).reshape(node_count, head_width)
    left_all = blocks[2].transpose(1, 0, 2).reshape(eig_all.shape[0], node_count)
    eig_term = left_all + jnp.sum(eig_weight[:, :, None] * totals[2], axis=0)
    returned = lax.all_to_all(
        jnp.stack([output_heads, query_grad_heads, key_grad_heads, value_grad_heads]),
        "node",
        split_axis=1,
        concat_axis=2,
        tiled=True,
    )
    query_grad_nodes = returned[1]
    key_grad_nodes = returned[2]
    value_grad_nodes = returned[3]
    grad_rows = (
        jnp.einsum("re,de->rd", query_grad_nodes, w_query, preferred_element_type=jnp.float32)
        + jnp.einsum("re,de->rd", key_grad_nodes, w_key, preferred_element_type=jnp.float32)
        + jnp.einsum("re,de->rd", value_grad_nodes, w_value, preferred_element_type=jnp.float32)
    ).astype(jnp.bfloat16)
    grad_eigvec = lax.psum_scatter(eig_term, "node", scatter_dimension=1, tiled=True)
    grad_weight = lax.psum(totals[3], "clus")
    rows_every, grads_every = (
        lax.all_gather(node_rows, "node", axis=0, tiled=True),
        lax.all_gather(grads_in, "node", axis=0, tiled=True),
    )
    grad_terms = jnp.stack(
        [
            jnp.einsum(
                "rd,re->de", rows_every, query_grad_heads, preferred_element_type=jnp.float32
            ),
            jnp.einsum("rd,re->de", rows_every, key_grad_heads, preferred_element_type=jnp.float32),
            jnp.einsum(
                "rd,re->de", rows_every, value_grad_heads, preferred_element_type=jnp.float32
            ),
            jnp.einsum("rd,re->de", grads_every, output_heads, preferred_element_type=jnp.float32),
        ]
    )
    grad_proj = lax.psum_scatter(grad_terms, "clus", scatter_dimension=1, tiled=True)
    return (grad_rows[None], grad_eigvec[None], grad_weight, grad_proj)


def solution(mesh):
    placed = (
        P("clus", "node", None),
        P("clus", "node", None),
        P(),
        P(),
        P(),
        P(),
        P("clus", None, None),
        P("node", None),
        P("clus", "node", None, None),
    )
    return jax.shard_map(
        body,
        mesh=mesh,
        in_specs=placed,
        out_specs=(
            P("clus", "node", None),
            P("clus", None, "node"),
            P("node", None),
            P(None, "clus", "node"),
        ),
        check_vma=False,
    )
```

profile of v0, /device:TPU:0, one launch (start us, length us, event | category | flops | bytes accessed | tf_op | source)
XLA Modules:
  0.0 163.7 jit_solution(6251420609520335516)
XLA Ops:
  10.3 2.1 %fusion.8 = bf16[1,128,1024]{2,1,0:T(8,128)(2,1)S(1)} fusion(bf16[1024,1024]{1,0:T(8,128)(2,1)} %param.12, bf16[1,128,1024]{2,1,0:T(8,128)(2,1)} %param.9), kind=kOutput, calls=%fused_computation.30 | convolution fusion | flops 268566528 | bytes 2621440 | tf_op jit(solution)/shard_map/dot_general | solution.py:11
  15.0 5.2 %all-to-all-start = ((bf16[4,128,1024]{1,0,2:T(4,128)(2,1)}), bf16[4,128,1024]{1,0,2:T(4,128)(2,1)S(1)}, u32[]{:S(2)}, u32[]{:S(2)}) async-start(bf16[4,128,1024]{1,0,2:T(4,128)(2,1)} %copy.56), calls=%async_computation | async-start | bytes 2097152 | tf_op jit(solution)/shard_map/all_to_all | solution.py:16
  22.7 4.4 %reshape.59 = pred[4,512,512]{1,2,0:T(32,128)(4,1)} reshape(pred[4,4,128,4,128]{2,1,4,3,0:T(4,128)(4,1)} %broadcast_in_dim.45) | data formatting | bytes 2097152 | tf_op jit(solution)/shard_map/while/body/eval_jaxpr/reshape | solution.py:63
  27.2 9.4 %all-to-all-done = bf16[4,128,1024]{1,0,2:T(4,128)(2,1)S(1)} async-done(((bf16[4,128,1024]{1,0,2:T(4,128)(2,1)}), bf16[4,128,1024]{1,0,2:T(4,128)(2,1)S(1)}, u32[]{:S(2)}, u32[]{:S(2)}) %all-to-all-start) | async-done | bytes 1048608 | tf_op jit(solution)/shard_map/all_to_all | solution.py:16
  42.2 1.8 %squeeze.35 = bf16[512,4,64]{0,2,1:T(8,128)(2,1)} reshape(bf16[1,4,128,256]{2,1,3,0:T(4,128)(2,1)} %get-tuple-element.76) | data formatting | bytes 524288 | tf_op jit(solution)/shard_map/squeeze | solution.py:28
  46.9 2.7 %fusion.28 = (f32[4,512]{1,0:T(4,128)S(1)}, f32[4,512,512]{1,2,0:T(8,128)S(1)}) fusion(f32[4,512,512]{1,2,0:T(8,128)S(1)} %fusion.1), kind=kOutput, calls=%fused_computation.59 | output fusion | flops 2097663 | bytes 8396800 | tf_op jit(solution)/shard_map/while/body/eval_jaxpr/sub | solution.py:66
  50.4 2.5 %multiply_convert_fusion = bf16[4,512,512]{1,2,0:T(8,128)(2,1)} fusion(f32[4,512,512]{1,2,0:T(8,128)S(1)} %get-tuple-element.80, f32[4,512]{1,0:T(4,128)S(1)} %get-tuple-element.79, f32[4,512,512]{1,2,0:T(8,128)S(1)} %get-tuple-element.78, f32[4,512]{1,0:T(4,128)S(1)} %get-tuple-element.77), kind=kLoop, calls=%fused_computation.4 | loop fusion | flops 4194304 | bytes 10502144 | tf_op jit(solution)/shard_map/while/body/eval_jaxpr/convert_element_type | solution.py:76
  52.9 5.5 %convolution_convert_fusion = bf16[4,64,512]{2,1,0:T(8,128)(2,1)} fusion(bf16[512,4,64]{0,2,1:T(8,128)(2,1)S(1)} %copy-done.18, f32[4,512]{1,0:T(4,128)S(1)} %get-tuple-element.77, f32[4,512,512]{1,2,0:T(8,128)} %copy-done.1), kind=kOutput, calls=%fused_computation.18 | convolution fusion | flops 137497088 | bytes 4726784 | tf_op jit(solution)/shard_map/while/body/eval_jaxpr/hij,ihd->jhd/dot_general | solution.py:84
  58.4 5.3 %convolution_convert_fusion.1 = bf16[4,64,512]{2,1,0:T(8,128)(2,1)} fusion(bf16[512,4,64]{0,2,1:T(8,128)(2,1)S(1)} %copy-done.17, f32[4,512]{1,0:T(4,128)S(1)} %get-tuple-element.77, f32[4,512,512]{1,2,0:T(8,128)} %copy-done.1), kind=kOutput, calls=%fused_computation.19 | convolution fusion | flops 137497088 | bytes 4726784 | tf_op jit(solution)/shard_map/while/body/eval_jaxpr/hij,jhd->ihd/dot_general | solution.py:69
  63.7 2.3 %fusion.3 = bf16[4,64,512]{2,1,0:T(8,128)(2,1)S(1)} fusion(bf16[512,4,64]{0,2,1:T(8,128)(2,1)S(1)} %copy-done.10, bf16[4,512,512]{1,2,0:T(8,128)(2,1)} %multiply_convert_fusion), kind=kOutput, calls=%fused_computation.25 | convolution fusion | flops 134479872 | bytes 2621440 | tf_op jit(solution)/shard_map/while/body/eval_jaxpr/hij,ihd->jhd/dot_general | solution.py:81
  66.1 2.9 %fusion.2 = bf16[4,64,512]{2,1,0:T(8,128)(2,1)} fusion(bf16[512,4,64]{0,2,1:T(8,128)(2,1)S(1)} %copy-done.9, bf16[4,512,512]{1,2,0:T(8,128)(2,1)} %multiply_convert_fusion), kind=kOutput, calls=%fused_computation.24 | convolution fusion | flops 134479872 | bytes 2621440 | tf_op jit(solution)/shard_map/while/body/eval_jaxpr/hij,jhd->ihd/dot_general | solution.py:78
  70.9 2.7 %convolution_bitcast_fusion.2 = f32[1,1024,256]{1,2,0:T(8,128)} fusion(bf16[512,256]{0,1:T(8,128)(2,1)S(1)} %bitcast.140, bf16[1,512,1024]{2,1,0:T(8,128)(2,1)} %all-gather.5.cloned.1.call-done), kind=kOutput, calls=%fused_computation.10 | convolution fusion | flops 268435456 | bytes 2359296 | tf_op jit(solution)/shard_map/rd,re->de/dot_general | solution.py:134
  76.8 3.9 %pad_maximum_fusion = f32[4,1024,256]{1,2,0:T(8,128)} fusion(f32[1,1024,256]{1,2,0:T(8,128)S(1)} %convolution_bitcast_fusion, f32[1,1024,256]{1,2,0:T(8,128)S(1)} %convolution_bitcast_fusion.1, f32[1,1024,256]{1,2,0:T(8,128)} %convolution_bitcast_fusion.2, f32[1,1024,256]{1,2,0:T(8,128)} %convolution_bitcast_fusion.3), kind=kLoop, calls=%fused_computation.1 | loop fusion | flops 3145728 | bytes 8388608 | tf_op jit(solution)/shard_map/stack | solution.py:129
  82.1 2.0 %copy.63 = bf16[1,512,256]{2,0,1:T(2,128)(2,1)} copy(bf16[1,512,256]{1,2,0:T(8,128)(2,1)} %bitcast.147) | data formatting | bytes 524288 | tf_op jit(solution)/shard_map/stack;reshape | solution.py:109
  85.8 4.6 %pad_maximum_fusion.2 = bf16[4,512,256]{2,0,1:T(4,128)(2,1)} fusion(bf16[1,512,256]{2,0,1:T(2,128)(2,1)S(1)} %copy.66, bf16[1,512,256]{2,0,1:T(2,128)(2,1)} %copy.65, bf16[1,512,256]{2,0,1:T(2,128)(2,1)S(1)} %copy.64, bf16[1,512,256]{2,0,1:T(2,128)(2,1)} %copy.63), kind=kLoop, calls=%fused_computation.34 | loop fusion | flops 4194304 | bytes 2097152 | tf_op jit(solution)/shard_map/stack | solution.py:109
  90.4 3.7 %all-to-all-start.1 = ((bf16[4,512,256]{2,0,1:T(4,128)(2,1)}), bf16[4,512,256]{2,0,1:T(4,128)(2,1)S(1)}, u32[]{:S(2)}, u32[]{:S(2)}) async-start(bf16[4,512,256]{2,0,1:T(4,128)(2,1)} %pad_maximum_fusion.2), calls=%async_computation.1 | async-start | bytes 2097152 | tf_op jit(solution)/shard_map/all_to_all | solution.py:108
  94.1 2.4 %fusion.5 = f32[512,64]{0,1:T(8,128)S(1)} fusion(bf16[4,512,512]{1,2,0:T(8,128)(2,1)} %multiply_convert_fusion, f32[4,64]{1,0:T(4,128)S(1)} %copy-done.19, bf16[1,64,512]{2,1,0:T(8,128)(2,1)} %param.15), kind=kOutput, calls=%fused_computation.27 | convolution fusion | flops 134447104 | bytes 2294784 | tf_op jit(solution)/shard_map/while/body/eval_jaxpr/hij,ki->hkj/dot_general | solution.py:89
  96.5 2.2 %multiply_reduce_fusion.1 = (f32[4,64]{1,0:T(4,128)S(1)}, f32[64,512]{1,0:T(8,128)S(1)}) fusion(f32[64,512]{1,0:T(8,128)S(1)} %bitcast_convert_fusion, f32[4,64]{1,0:T(4,128)S(1)} %copy-done.19, bf16[4,512,512]{1,2,0:T(8,128)(2,1)} %multiply_convert_fusion, bf16[1,64,512]{2,1,0:T(8,128)(2,1)S(1)} %copy-done.15), kind=kOutput, calls=%fused_computation.42 | convolution fusion | flops 134708992 | bytes 2426880 | tf_op jit(solution)/shard_map/while/body/eval_jaxpr/hij,kj->hki/dot_general | solution.py:87
  99.4 17.7 %psum.7 = f32[4,64]{1,0:T(4,128)} all-reduce(f32[4,64]{1,0:T(4,128)S(1)} %get-tuple-element.68), channel_id=1, replica_groups=mesh['clus'=8,'node'=4] {'clus'}, use_global_device_ids=true, to_apply=%region_7.8 | all-reduce | flops 256 | bytes 2048 | tf_op jit(solution)/shard_map/psum | solution.py:124
  118.5 2.4 %convolution_add_fusion.1 = f32[128,1024]{1,0:T(8,128)S(1)} fusion(f32[128,1024]{1,0:T(8,128)S(1)} %fusion.30, bf16[128,1024]{0,1:T(8,128)(2,1)S(1)} %bitcast.149, bf16[1024,1024]{1,0:T(8,128)(2,1)} %param.12), kind=kOutput, calls=%fused_computation.15 | convolution fusion | flops 268566528 | bytes 3407872 | tf_op jit(solution)/shard_map/re,de->rd/dot_general | solution.py:120
  121.2 3.2 %fusion.6 = bf16[1,128,1024]{2,1,0:T(8,128)(2,1)} fusion(f32[128,1024]{1,0:T(8,128)S(1)} %convolution_add_fusion.1, bf16[128,1024]{0,1:T(8,128)(2,1)S(1)} %bitcast.148, bf16[1024,1024]{1,0:T(8,128)(2,1)} %param.13), kind=kOutput, calls=%fused_computation.28 | convolution fusion | flops 268697600 | bytes 3145728 | tf_op jit(solution)/shard_map/re,de->rd/dot_general | solution.py:121
  124.3 7.0 %reduce-scatter.5.cloned.1.call-done = f32[4,128,256]{1,2,0:T(8,128)} async-done(((f32[4,1024,256]{1,2,0:T(8,128)}), f32[4,128,256]{1,2,0:T(8,128)}) %reduce-scatter.5.cloned.1.call-update) | async-done | bytes 524304 | tf_op jit(solution)/shard_map/reduce_scatter | solution.py:141
  131.4 2.0 %copy.73 = f32[4,128,256]{2,1,0:T(8,128)} copy(f32[4,128,256]{1,2,0:T(8,128)} %reduce-scatter.5.cloned.1.call-done) | data formatting | bytes 1048576
  133.4 23.8 %reduce-scatter.3.cloned.1.call-done = f32[64,128]{1,0:T(8,128)} async-done(((f32[64,512]{1,0:T(8,128)}), f32[64,128]{1,0:T(8,128)}) %reduce-scatter.3.cloned.1.call-update) | async-done | bytes 32784 | tf_op jit(solution)/shard_map/reduce_scatter | solution.py:123
  (83 shorter events, 27.6 us)
Async XLA Ops:
  7.2 5.3 %copy-start.4 = (bf16[1,128,1024]{2,1,0:T(8,128)(2,1)S(1)}, bf16[1,128,1024]{2,1,0:T(8,128)(2,1)}, u32[]{:S(2)}) copy-start(bf16[1,128,1024]{2,1,0:T(8,128)(2,1)} %param.9) | copy-start | bytes 786436
  7.2 5.7 %copy-start.16 = (bf16[1,128,1024]{2,1,0:T(8,128)(2,1)S(1)}, bf16[1,128,1024]{2,1,0:T(8,128)(2,1)}, u32[]{:S(2)}) copy-start(bf16[1,128,1024]{2,1,0:T(8,128)(2,1)} %param.10) | copy-start | bytes 786436
  7.2 61.8 %all-gather.5.cloned.1.call-start = ((), (), s32[]{:S(2)}) async-start(), calls=%async_computation.6 | async-start | bytes 1310720 | tf_op jit(solution)/shard_map/all_gather | solution.py:126
  8.8 3.7 %copy-start.3 = (bf16[1024,1024]{1,0:T(8,128)(2,1)S(1)}, bf16[1024,1024]{1,0:T(8,128)(2,1)}, u32[]{:S(2)}) copy-start(bf16[1024,1024]{1,0:T(8,128)(2,1)} %param.13) | copy-start | bytes 6291460
  8.8 4.2 %copy-start.11 = (bf16[1024,1024]{1,0:T(8,128)(2,1)S(1)}, bf16[1024,1024]{1,0:T(8,128)(2,1)}, u32[]{:S(2)}) copy-start(bf16[1024,1024]{1,0:T(8,128)(2,1)} %param.14) | copy-start | bytes 6291460
  13.0 8.0 %copy-start.20 = (s32[1,4,4,4]{3,2,1,0:T(4,128)S(1)}, s32[1,4,4,4]{3,2,1,0:T(4,128)}, u32[]{:S(2)}) copy-start(s32[1,4,4,4]{3,2,1,0:T(4,128)} %param.17) | copy-start | bytes 772
  13.6 13.6 %copy-start.13 = (bf16[1,64,512]{2,1,0:T(8,128)(2,1)S(1)}, bf16[1,64,512]{2,1,0:T(8,128)(2,1)}, u32[]{:S(2)}) copy-start(bf16[1,64,512]{2,1,0:T(8,128)(2,1)} %param.15) | copy-start | bytes 196612
  15.0 21.6 %all-to-all-start = ((bf16[4,128,1024]{1,0,2:T(4,128)(2,1)}), bf16[4,128,1024]{1,0,2:T(4,128)(2,1)S(1)}, u32[]{:S(2)}, u32[]{:S(2)}) async-start(bf16[4,128,1024]{1,0,2:T(4,128)(2,1)} %copy.56), calls=%async_computation | async-start | bytes 2097152 | tf_op jit(solution)/shard_map/all_to_all | solution.py:16
  20.2 54.8 %all-gather.7.cloned.1.call-start = ((), (), s32[]{:S(2)}) async-start(), calls=%async_computation.7 | async-start | bytes 1310720 | tf_op jit(solution)/shard_map/all_gather | solution.py:127
  20.9 110.4 %reduce-scatter.5.cloned.1.call-start = ((), (), s32[]{:S(2)}) async-start(), calls=%async_computation.5 | async-start | bytes 4718592 | tf_op jit(solution)/shard_map/reduce_scatter | solution.py:141
  37.4 8.4 %copy-start.5 = (pred[4,512,512]{1,2,0:T(32,128)(4,1)S(1)}, pred[4,512,512]{1,2,0:T(32,128)(4,1)}, u32[]{:S(2)}) copy-start(pred[4,512,512]{1,2,0:T(32,128)(4,1)} %reshape.59) | copy-start | bytes 3145732
  37.4 8.4 %copy-start.19 = (f32[4,64]{1,0:T(4,128)S(1)}, f32[4,64]{1,0:T(4,128)}, u32[]{:S(2)}) copy-start(f32[4,64]{1,0:T(4,128)} %param.16) | copy-start | bytes 3076
  42.2 4.6 %copy-start.8 = (bf16[512,4,64]{0,2,1:T(8,128)(2,1)}, bf16[512,4,64]{0,2,1:T(8,128)(2,1)S(1)}, u32[]{:S(2)}) copy-start(bf16[512,4,64]{0,2,1:T(8,128)(2,1)S(1)} %squeeze.36) | copy-start | bytes 786436
  46.8 2.7 %copy-start.1 = (f32[4,512,512]{1,2,0:T(8,128)}, f32[4,512,512]{1,2,0:T(8,128)S(1)}, u32[]{:S(2)}) copy-start(f32[4,512,512]{1,2,0:T(8,128)S(1)} %fusion.1) | copy-start | bytes 12582916
  46.9 2.7 %copy-start.17 = (bf16[512,4,64]{0,2,1:T(8,128)(2,1)S(1)}, bf16[512,4,64]{0,2,1:T(8,128)(2,1)}, u32[]{:S(2)}) copy-start(bf16[512,4,64]{0,2,1:T(8,128)(2,1)} %squeeze.34) | copy-start | bytes 786436
  46.9 2.7 %copy-start.18 = (bf16[512,4,64]{0,2,1:T(8,128)(2,1)S(1)}, bf16[512,4,64]{0,2,1:T(8,128)(2,1)}, u32[]{:S(2)}) copy-start(bf16[512,4,64]{0,2,1:T(8,128)(2,1)} %squeeze.37) | copy-start | bytes 786436
  58.4 5.3 %copy-start.10 = (bf16[512,4,64]{0,2,1:T(8,128)(2,1)S(1)}, bf16[512,4,64]{0,2,1:T(8,128)(2,1)}, u32[]{:S(2)}) copy-start(bf16[512,4,64]{0,2,1:T(8,128)(2,1)} %squeeze.35) | copy-start | bytes 786436
  58.4 7.7 %copy-start.9 = (bf16[512,4,64]{0,2,1:T(8,128)(2,1)S(1)}, bf16[512,4,64]{0,2,1:T(8,128)(2,1)}, u32[]{:S(2)}) copy-start(bf16[512,4,64]{0,2,1:T(8,128)(2,1)} %copy-done.8) | copy-start | bytes 786436
  69.0 4.6 %copy-start.2 = (bf16[1,512,1024]{2,1,0:T(8,128)(2,1)S(1)}, bf16[1,512,1024]{2,1,0:T(8,128)(2,1)}, u32[]{:S(2)}) copy-start(bf16[1,512,1024]{2,1,0:T(8,128)(2,1)} %all-gather.5.cloned.1.call-done) | copy-start | bytes 3145732
  69.0 4.6 %copy-start.6 = (bf16[4,64,512]{2,1,0:T(8,128)(2,1)S(1)}, bf16[4,64,512]{2,1,0:T(8,128)(2,1)}, u32[]{:S(2)}) copy-start(bf16[4,64,512]{2,1,0:T(8,128)(2,1)} %fusion.2) | copy-start | bytes 786436
  80.7 4.5 %copy-start.7 = (bf16[4,64,512]{2,1,0:T(8,128)(2,1)S(1)}, bf16[4,64,512]{2,1,0:T(8,128)(2,1)}, u32[]{:S(2)}) copy-start(bf16[4,64,512]{2,1,0:T(8,128)(2,1)} %fusion.2) | copy-start | bytes 786436
  90.4 6.1 %copy-start.15 = (bf16[1,64,512]{2,1,0:T(8,128)(2,1)S(1)}, bf16[1,64,512]{2,1,0:T(8,128)(2,1)}, u32[]{:S(2)}) copy-start(bf16[1,64,512]{2,1,0:T(8,128)(2,1)} %param.15) | copy-start | bytes 196612
  90.4 26.7 %all-to-all-start.1 = ((bf16[4,512,256]{2,0,1:T(4,128)(2,1)}), bf16[4,512,256]{2,0,1:T(4,128)(2,1)S(1)}, u32[]{:S(2)}, u32[]{:S(2)}) async-start(bf16[4,512,256]{2,0,1:T(4,128)(2,1)} %pad_maximum_fusion.2), calls=%async_computation.1 | async-start | bytes 2097152 | tf_op jit(solution)/shard_map/all_to_all | solution.py:108
  94.1 63.1 %reduce-scatter.3.cloned.1.call-start = ((), (), s32[]{:S(2)}) async-start(), calls=%async_computation.4 | async-start | bytes 163840 | tf_op jit(solution)/shard_map/reduce_scatter | solution.py:123
  (3 other events, 4.3 us)
Sparse Core Ops, SparseCore 0:
  9.9 36.7 all-gather.4
  48.5 26.5 all-gather.6
  80.9 50.4 reduce-scatter.4
  134.5 22.6 reduce-scatter.2
where the time goes:
time: 165 us; the launch traced here: 164 us
  matrix products  42.9 us (26%)
  waiting for transfers between devices  41.7 us (25%)
  local copies, waits for them, and re-layouts  23.7 us (14%)
  blocking collectives  17.7 us (11%)
  other arithmetic  14.6 us (9%)
  between operations  14.1 us (9%)
  starting transfers between devices  8.96 us (5%)
    reduce_scatter x1, waiting for transfers between devices, body(): lax.psum_scatter(eig_term, 'node', scatter_dimension=1, tiled=True)  23.8 us
    psum x1, blocking collectives, body(): grad_weight = lax.psum(totals[3], 'clus')  17.7 us
    all_to_all x1, waiting for transfers between devices, body(): lax.all_to_all(jnp.stack([query, keys_local, values_local, d_att]), 'node...  9.41 us
    reduce_scatter x1, waiting for transfers between devices, body(): lax.psum_scatter(grad_terms, 'clus', scatter_dimension=1, tiled=True)  7.05 us
    dot_general x1, matrix products, one_block(): jnp.einsum('hij,ihd->jhd', prob_half, dout_block, preferred_element_type=...  5.48 us
    dot_general x1, matrix products, one_block(): jnp.einsum('hij,jhd->ihd', prob_half, values_heads, preferred_element_typ...  5.33 us
    all_to_all x1, starting transfers between devices, body(): lax.all_to_all(jnp.stack([query, keys_local, values_local, d_att]), 'node...  5.19 us
    another operation x1, other arithmetic, body(): jnp.stack([output_heads, query_grad_heads, key_grad_heads, value_grad_hea...  4.64 us
  transfers between devices with their start and end apart: 6, of which 3 were waited for; matrix products, arithmetic and copies ran while one was open for 45% of the time, Pallas kernels for 0%

commit v1 on v0

--- a/solution.py
+++ b/solution.py
@@ -2,6 +2,17 @@
 import jax.numpy as jnp
 from jax import lax
 from jax.sharding import PartitionSpec as P
+
+
+def split_up(x, dim, size):
+    before, after = (x.shape[:dim], x.shape[dim + 1 :])
+    return jnp.moveaxis(x.reshape(*before, size, -1, *after), dim, 0)
+
+
+def joined_along(parts, dim):
+    parts = jnp.moveaxis(parts, 0, dim)
+    shape = parts.shape
+    return parts.reshape(*shape[:dim], shape[dim] * shape[dim + 1], *shape[dim + 2 :])
 
 
 def body(node_feats, cotangent, w_query, w_key, w_value, w_out, eigvec, eig_weight, block_mask):
@@ -13,13 +24,15 @@
         jnp.bfloat16
     )
     d_att = jnp.dot(grads_in, w_out, preferred_element_type=jnp.float32).astype(jnp.bfloat16)
-    head_data = lax.all_to_all(
-        jnp.stack([query, keys_local, values_local, d_att]),
-        "node",
-        split_axis=2,
-        concat_axis=1,
-        tiled=True,
-    )
+    value = jnp.stack([query, keys_local, values_local, d_att])
+    peers, index = (lax.axis_size("node"), lax.axis_index("node"))
+    blocks_2 = split_up(value, 2, peers)
+    gathered = [blocks_2[index]]
+    for step in range(1, peers):
+        sent = blocks_2[index ^ step]
+        gathered.append(lax.ppermute(sent, "node", [(i, i ^ step) for i in range(peers)]))
+    blocks_2 = jnp.stack(gathered)[index ^ jnp.arange(peers)]
+    head_data = joined_along(blocks_2, 1)
     node_count = head_data.shape[1]
     head_width = head_data.shape[2]
     heads_dev = eig_weight.shape[0]

time: 165 us -> 182 us (1.10)
  local copies, waits for them, and re-layouts: 23.7 us -> 32 us
  waiting for transfers between devices: 41.7 us -> 45.6 us
  matrix products: 42.9 us -> 45.6 us
  other arithmetic: 14.6 us -> 16.8 us
    ppermute x0 -> x3, waiting for transfers between devices: none -> 13.5 us  [body(): lax.ppermute(sent, 'node', [(i, i ^ step) for i in range(peers)])]
    all_to_all x1 -> x0, waiting for transfers between devices: 9.41 us -> none  [body(): lax.all_to_all(jnp.stack([query, keys_local, values_local, d_att]), 'node...]
    all_to_all x1 -> x0, starting transfers between devices: 5.19 us -> none  [body(): lax.all_to_all(jnp.stack([query, keys_local, values_local, d_att]), 'node...]
    slice x0 -> x3, local copies, waits for them, and re-layouts: none -> 4.87 us  [the longest x1 1.91 us: body(): query_heads = by_head[0]]
    ppermute x0 -> x3, starting transfers between devices: none -> 4.47 us  [body(): lax.ppermute(sent, 'node', [(i, i ^ step) for i in range(peers)])]
    another operation x1, other arithmetic: 0.13 us -> 2.34 us  [body(): blocks_2 = jnp.stack(gathered)[index ^ jnp.arange(peers)]]
    unnamed x43 -> x40, local copies, waits for them, and re-layouts: 3.88 us -> 6.01 us
    gather x0 -> x1, local copies, waits for them, and re-layouts: none -> 1.84 us  [body(): blocks_2 = jnp.stack(gathered)[index ^ jnp.arange(peers)]]
  transfers between devices with their start and end apart: 6 -> 8, of which waited for: 3 -> 5; matrix products, arithmetic and copies ran while one was open for 45% -> 49% of each run, Pallas kernels for 0% -> 0%
where the time goes in v1:
time: 182 us; the launch traced here: 181 us
  waiting for transfers between devices  45.6 us (25%)
  matrix products  45.6 us (25%)
  local copies, waits for them, and re-layouts  32 us (18%)
  blocking collectives  18 us (10%)
  other arithmetic  16.8 us (9%)
  between operations  14.2 us (8%)
  starting transfers between devices  8.27 us (5%)
    reduce_scatter x1, waiting for transfers between devices, body(): lax.psum_scatter(eig_term, 'node', scatter_dimension=1, tiled=True)  23.8 us
    psum x1, blocking collectives, body(): grad_weight = lax.psum(totals[3], 'clus')  18 us
    ppermute x3, waiting for transfers between devices, body(): lax.ppermute(sent, 'node', [(i, i ^ step) for i in range(peers)])  13.5 us
    reduce_scatter x1, waiting for transfers between devices, body(): lax.psum_scatter(grad_terms, 'clus', scatter_dimension=1, tiled=True)  6.97 us
    unnamed x40, local copies, waits for them, and re-layouts  6.01 us
    dot_general x1, matrix products, one_block(): jnp.einsum('hij,jhd->ihd', prob_half, values_heads, preferred_element_typ...  5.33 us
    dot_general x1, matrix products, one_block(): jnp.einsum('hij,ihd->jhd', prob_half, dout_block, preferred_element_type=...  5.29 us
    another operation x1, other arithmetic, body(): jnp.stack([output_heads, query_grad_heads, key_grad_heads, value_grad_hea...  4.63 us
  transfers between devices with their start and end apart: 8, of which 5 were waited for; matrix products, arithmetic and copies ran while one was open for 49% of the time, Pallas kernels for 0%

profile of v1, /device:TPU:0, one launch (start us, length us, event | category | flops | bytes accessed | tf_op | source)
XLA Modules:
  0.0 180.5 jit_solution(15113855946306491890)
XLA Ops:
  8.7 2.1 %convolution_convert_fusion.2 = bf16[128,1024]{1,0:T(8,128)(2,1)S(1)} fusion(bf16[1024,1024]{1,0:T(8,128)(2,1)} %param.14, bf16[1,128,1024]{2,1,0:T(8,128)(2,1)} %param.10), kind=kOutput, calls=%fused_computation.21 | convolution fusion | flops 268566528 | bytes 2621440 | tf_op jit(solution)/shard_map/dot_general | solution.py:26
  13.4 2.0 %convolution_convert_fusion.4 = bf16[128,1024]{1,0:T(8,128)(2,1)S(1)} fusion(bf16[1024,1024]{1,0:T(8,128)(2,1)} %param.12, bf16[1,128,1024]{2,1,0:T(8,128)(2,1)S(1)} %copy-done.3), kind=kOutput, calls=%fused_computation.23 | convolution fusion | flops 268566528 | bytes 2621440 | tf_op jit(solution)/shard_map/dot_general | solution.py:22
  23.3 3.9 %collective-permute-start.2 = (bf16[4,128,256]{2,1,0:T(8,128)(2,1)}, bf16[4,128,256]{2,1,0:T(8,128)(2,1)}, u32[]{:S(2)}, u32[]{:S(2)}) collective-permute-start(bf16[4,128,256]{2,1,0:T(8,128)(2,1)} %get-tuple-element.78), channel_id=1, source_target_pairs={{0,3},{1,2},{2,1},{3,0},{4,7},{5,6},{6,5},{7,4},{8,11},{9,10},{10,... | collective-permute-start | bytes 786440 | tf_op jit(solution)/shard_map/ppermute | solution.py:33
  28.5 3.3 %reshape.89 = pred[4,512,512]{1,2,0:T(32,128)(4,1)} reshape(pred[4,4,128,4,128]{2,1,4,3,0:T(4,128)(4,1)S(1)} %broadcast_in_dim.46) | data formatting | bytes 2097152 | tf_op jit(solution)/shard_map/while/body/eval_jaxpr/reshape | solution.py:76
  31.9 5.3 %collective-permute-done.2 = bf16[4,128,256]{2,1,0:T(8,128)(2,1)} collective-permute-done((bf16[4,128,256]{2,1,0:T(8,128)(2,1)}, bf16[4,128,256]{2,1,0:T(8,128)(2,1)}, u32[]{:S(2)}, u32[]{:S(2)}) %collective-permute-start.2) | collective-permute-done | bytes 262176 | tf_op jit(solution)/shard_map/ppermute | solution.py:33
  37.2 7.7 %collective-permute-done.1 = bf16[4,128,256]{2,1,0:T(8,128)(2,1)} collective-permute-done((bf16[4,128,256]{2,1,0:T(8,128)(2,1)}, bf16[4,128,256]{2,1,0:T(8,128)(2,1)}, u32[]{:S(2)}, u32[]{:S(2)}) %collective-permute-start.1) | collective-permute-done | bytes 262176 | tf_op jit(solution)/shard_map/ppermute | solution.py:33
  45.3 2.3 %pad_maximum_fusion.1 = bf16[4,4,128,256]{3,2,1,0:T(8,128)(2,1)} fusion(bf16[1,4,128,256]{3,2,1,0:T(8,128)(2,1)} %bitcast.8, bf16[1,4,128,256]{3,2,1,0:T(8,128)(2,1)} %bitcast.6, bf16[1,4,128,256]{3,2,1,0:T(8,128)(2,1)} %bitcast.4, bf16[1,4,128,256]{3,2,1,0:T(8,128)(2,1)} %get-tuple-element.77), kind=kLoop, calls=%fused_computation.30 | loop fusion | flops 1572864 | bytes 2097152 | tf_op jit(solution)/shard_map/stack | solution.py:34
  63.8 2.7 %fusion.25 = (f32[4,512]{1,0:T(4,128)S(1)}, f32[4,512,512]{1,2,0:T(8,128)S(1)}) fusion(f32[4,512,512]{1,2,0:T(8,128)S(1)} %fusion.1), kind=kOutput, calls=%fused_computation.66 | output fusion | flops 2097663 | bytes 8396800 | tf_op jit(solution)/shard_map/while/body/eval_jaxpr/sub | solution.py:79
  67.3 2.5 %multiply_convert_fusion = bf16[4,512,512]{1,2,0:T(8,128)(2,1)} fusion(f32[4,512,512]{1,2,0:T(8,128)S(1)} %get-tuple-element.84, f32[4,512]{1,0:T(4,128)S(1)} %get-tuple-element.83, f32[4,512,512]{1,2,0:T(8,128)S(1)} %get-tuple-element.82, f32[4,512]{1,0:T(4,128)S(1)} %get-tuple-element.81), kind=kLoop, calls=%fused_computation.5 | loop fusion | flops 4194304 | bytes 10502144 | tf_op jit(solution)/shard_map/while/body/eval_jaxpr/convert_element_type | solution.py:89
  69.8 5.3 %convolution_convert_fusion = bf16[4,64,512]{2,1,0:T(8,128)(2,1)} fusion(bf16[512,4,64]{0,2,1:T(8,128)(2,1)S(1)} %copy-done.15, f32[4,512]{1,0:T(4,128)S(1)} %get-tuple-element.81, f32[4,512,512]{1,2,0:T(8,128)} %copy-done.1), kind=kOutput, calls=%fused_computation.19 | convolution fusion | flops 137497088 | bytes 4726784 | tf_op jit(solution)/shard_map/while/body/eval_jaxpr/hij,ihd->jhd/dot_general | solution.py:97
  75.1 5.3 %convolution_convert_fusion.1 = bf16[4,64,512]{2,1,0:T(8,128)(2,1)} fusion(bf16[512,4,64]{0,2,1:T(8,128)(2,1)S(1)} %copy-done.14, f32[4,512]{1,0:T(4,128)S(1)} %get-tuple-element.81, f32[4,512,512]{1,2,0:T(8,128)} %copy-done.1), kind=kOutput, calls=%fused_computation.20 | convolution fusion | flops 137497088 | bytes 4726784 | tf_op jit(solution)/shard_map/while/body/eval_jaxpr/hij,jhd->ihd/dot_general | solution.py:82
  80.5 2.3 %fusion.3 = bf16[4,64,512]{2,1,0:T(8,128)(2,1)S(1)} fusion(bf16[512,4,64]{0,2,1:T(8,128)(2,1)S(1)} %copy-done.9, bf16[4,512,512]{1,2,0:T(8,128)(2,1)} %multiply_convert_fusion), kind=kOutput, calls=%fused_computation.26 | convolution fusion | flops 134479872 | bytes 2621440 | tf_op jit(solution)/shard_map/while/body/eval_jaxpr/hij,ihd->jhd/dot_general | solution.py:94
  82.8 2.8 %fusion.2 = bf16[4,64,512]{2,1,0:T(8,128)(2,1)} fusion(bf16[512,4,64]{0,2,1:T(8,128)(2,1)S(1)} %copy-done.8, bf16[4,512,512]{1,2,0:T(8,128)(2,1)} %multiply_convert_fusion), kind=kOutput, calls=%fused_computation.25 | convolution fusion | flops 134479872 | bytes 2621440 | tf_op jit(solution)/shard_map/while/body/eval_jaxpr/hij,jhd->ihd/dot_general | solution.py:91
  87.4 2.7 %convolution_bitcast_fusion.2 = f32[1,1024,256]{1,2,0:T(8,128)} fusion(bf16[512,256]{0,1:T(8,128)(2,1)S(1)} %bitcast.141, bf16[1,512,1024]{2,1,0:T(8,128)(2,1)} %all-gather.5.cloned.1.call-done), kind=kOutput, calls=%fused_computation.11 | convolution fusion | flops 268435456 | bytes 2359296 | tf_op jit(solution)/shard_map/rd,re->de/dot_general | solution.py:147
  93.4 3.9 %pad_maximum_fusion = f32[4,1024,256]{1,2,0:T(8,128)} fusion(f32[1,1024,256]{1,2,0:T(8,128)S(1)} %convolution_bitcast_fusion, f32[1,1024,256]{1,2,0:T(8,128)S(1)} %convolution_bitcast_fusion.1, f32[1,1024,256]{1,2,0:T(8,128)} %convolution_bitcast_fusion.2, f32[1,1024,256]{1,2,0:T(8,128)} %convolution_bitcast_fusion.3), kind=kLoop, calls=%fused_computation.2 | loop fusion | flops 3145728 | bytes 8388608 | tf_op jit(solution)/shard_map/stack | solution.py:142
  102.4 4.6 %pad_maximum_fusion.2 = bf16[4,512,256]{2,0,1:T(4,128)(2,1)} fusion(bf16[1,512,256]{2,0,1:T(2,128)(2,1)S(1)} %copy.76, bf16[1,512,256]{2,0,1:T(2,128)(2,1)} %copy.75, bf16[1,512,256]{2,0,1:T(2,128)(2,1)S(1)} %copy.74, bf16[1,512,256]{2,0,1:T(2,128)(2,1)} %copy.73), kind=kLoop, calls=%fused_computation.31 | loop fusion | flops 4194304 | bytes 2097152 | tf_op jit(solution)/shard_map/stack | solution.py:122
  107.0 3.6 %all-to-all-start = ((bf16[4,512,256]{2,0,1:T(4,128)(2,1)}), bf16[4,512,256]{2,0,1:T(4,128)(2,1)S(1)}, u32[]{:S(2)}, u32[]{:S(2)}) async-start(bf16[4,512,256]{2,0,1:T(4,128)(2,1)} %pad_maximum_fusion.2), calls=%async_computation | async-start | bytes 2097152 | tf_op jit(solution)/shard_map/all_to_all | solution.py:121
  110.7 2.4 %fusion.5 = f32[512,64]{0,1:T(8,128)S(1)} fusion(bf16[4,512,512]{1,2,0:T(8,128)(2,1)} %multiply_convert_fusion, f32[4,64]{1,0:T(4,128)S(1)} %copy-done.16, bf16[1,64,512]{2,1,0:T(8,128)(2,1)} %param.15), kind=kOutput, calls=%fused_computation.28 | convolution fusion | flops 134447104 | bytes 2294784 | tf_op jit(solution)/shard_map/while/body/eval_jaxpr/hij,ki->hkj/dot_general | solution.py:102
  113.1 2.2 %multiply_reduce_fusion.1 = (f32[4,64]{1,0:T(4,128)S(1)}, f32[64,512]{1,0:T(8,128)S(1)}) fusion(f32[64,512]{1,0:T(8,128)S(1)} %bitcast_convert_fusion, f32[4,64]{1,0:T(4,128)S(1)} %copy-done.16, bf16[4,512,512]{1,2,0:T(8,128)(2,1)} %multiply_convert_fusion, bf16[1,64,512]{2,1,0:T(8,128)(2,1)S(1)} %copy-done.13), kind=kOutput, calls=%fused_computation.38 | convolution fusion | flops 134708992 | bytes 2426880 | tf_op jit(solution)/shard_map/while/body/eval_jaxpr/hij,kj->hki/dot_general | solution.py:100
  116.0 18.0 %psum.7 = f32[4,64]{1,0:T(4,128)} all-reduce(f32[4,64]{1,0:T(4,128)S(1)} %get-tuple-element.68), channel_id=1, replica_groups=mesh['clus'=8,'node'=4] {'clus'}, use_global_device_ids=true, to_apply=%region_7.8 | all-reduce | flops 256 | bytes 2048 | tf_op jit(solution)/shard_map/psum | solution.py:137
  135.4 2.4 %convolution_add_fusion.1 = f32[128,1024]{1,0:T(8,128)S(1)} fusion(f32[128,1024]{1,0:T(8,128)S(1)} %fusion.27, bf16[128,1024]{0,1:T(8,128)(2,1)S(1)} %bitcast.150, bf16[1024,1024]{1,0:T(8,128)(2,1)} %param.12), kind=kOutput, calls=%fused_computation.16 | convolution fusion | flops 268566528 | bytes 3407872 | tf_op jit(solution)/shard_map/re,de->rd/dot_general | solution.py:133
  138.0 3.2 %fusion.6 = bf16[1,128,1024]{2,1,0:T(8,128)(2,1)} fusion(f32[128,1024]{1,0:T(8,128)S(1)} %convolution_add_fusion.1, bf16[128,1024]{0,1:T(8,128)(2,1)S(1)} %bitcast.149, bf16[1024,1024]{1,0:T(8,128)(2,1)} %param.13), kind=kOutput, calls=%fused_computation.29 | convolution fusion | flops 268697600 | bytes 3145728 | tf_op jit(solution)/shard_map/re,de->rd/dot_general | solution.py:134
  141.2 7.0 %reduce-scatter.5.cloned.1.call-done = f32[4,128,256]{1,2,0:T(8,128)} async-done(((f32[4,1024,256]{1,2,0:T(8,128)}), f32[4,128,256]{1,2,0:T(8,128)}) %reduce-scatter.5.cloned.1.call-update) | async-done | bytes 524304 | tf_op jit(solution)/shard_map/reduce_scatter | solution.py:154
  150.2 23.8 %reduce-scatter.3.cloned.1.call-done = f32[64,128]{1,0:T(8,128)} async-done(((f32[64,512]{1,0:T(8,128)}), f32[64,128]{1,0:T(8,128)}) %reduce-scatter.3.cloned.1.call-update) | async-done | bytes 32784 | tf_op jit(solution)/shard_map/reduce_scatter | solution.py:136
  (95 shorter events, 44.7 us)
Async XLA Ops:
  7.2 3.9 %copy-start = (bf16[1024,1024]{1,0:T(8,128)(2,1)S(1)}, bf16[1024,1024]{1,0:T(8,128)(2,1)}, u32[]{:S(2)}) copy-start(bf16[1024,1024]{1,0:T(8,128)(2,1)} %param.11) | copy-start | bytes 6291460
  7.2 6.2 %copy-start.3 = (bf16[1,128,1024]{2,1,0:T(8,128)(2,1)S(1)}, bf16[1,128,1024]{2,1,0:T(8,128)(2,1)}, u32[]{:S(2)}) copy-start(bf16[1,128,1024]{2,1,0:T(8,128)(2,1)} %param.9) | copy-start | bytes 786436
  7.2 78.4 %all-gather.5.cloned.1.call-start = ((), (), s32[]{:S(2)}) async-start(), calls=%async_computation.5 | async-start | bytes 1310720 | tf_op jit(solution)/shard_map/all_gather | solution.py:139
  7.9 83.7 %all-gather.7.cloned.1.call-start = ((), (), s32[]{:S(2)}) async-start(), calls=%async_computation.6 | async-start | bytes 1310720 | tf_op jit(solution)/shard_map/all_gather | solution.py:140
  8.7 139.5 %reduce-scatter.5.cloned.1.call-start = ((), (), s32[]{:S(2)}) async-start(), calls=%async_computation.4 | async-start | bytes 4718592 | tf_op jit(solution)/shard_map/reduce_scatter | solution.py:154
  15.4 12.3 %copy-start.17 = (s32[1,4,4,4]{3,2,1,0:T(4,128)S(1)}, s32[1,4,4,4]{3,2,1,0:T(4,128)}, u32[]{:S(2)}) copy-start(s32[1,4,4,4]{3,2,1,0:T(4,128)} %param.17) | copy-start | bytes 772
  18.3 13.5 %copy-start.11 = (bf16[1,64,512]{2,1,0:T(8,128)(2,1)S(1)}, bf16[1,64,512]{2,1,0:T(8,128)(2,1)}, u32[]{:S(2)}) copy-start(bf16[1,64,512]{2,1,0:T(8,128)(2,1)} %param.15) | copy-start | bytes 196612
  23.3 13.9 %collective-permute-start.2 = (bf16[4,128,256]{2,1,0:T(8,128)(2,1)}, bf16[4,128,256]{2,1,0:T(8,128)(2,1)}, u32[]{:S(2)}, u32[]{:S(2)}) collective-permute-start(bf16[4,128,256]{2,1,0:T(8,128)(2,1)} %get-tuple-element.78), channel_id=1, source_target_pairs={{0,3},{1,2},{2,1},{3,0},{4,7},{5,6},{6,5},{7,4},{8,11},{9,10},{10,... | collective-permute-start | bytes 786440 | tf_op jit(solution)/shard_map/ppermute | solution.py:33
  27.2 17.8 %collective-permute-start.1 = (bf16[4,128,256]{2,1,0:T(8,128)(2,1)}, bf16[4,128,256]{2,1,0:T(8,128)(2,1)}, u32[]{:S(2)}, u32[]{:S(2)}) collective-permute-start(bf16[4,128,256]{2,1,0:T(8,128)(2,1)} %get-tuple-element.79), channel_id=1, source_target_pairs={{0,2},{1,3},{2,0},{3,1},{4,6},{5,7},{6,4},{7,5},{8,10},{9,11},{10,... | collective-permute-start | bytes 786440 | tf_op jit(solution)/shard_map/ppermute | solution.py:33
  27.7 17.7 %collective-permute-start = (bf16[4,128,256]{2,1,0:T(8,128)(2,1)}, bf16[4,128,256]{2,1,0:T(8,128)(2,1)}, u32[]{:S(2)}, u32[]{:S(2)}) collective-permute-start(bf16[4,128,256]{2,1,0:T(8,128)(2,1)} %get-tuple-element.80), channel_id=1, source_target_pairs={{0,1},{1,0},{2,3},{3,2},{4,5},{5,4},{6,7},{7,6},{8,9},{9,8},{10,11... | collective-permute-start | bytes 786440 | tf_op jit(solution)/shard_map/ppermute | solution.py:33
  51.6 11.1 %copy-start.4 = (pred[4,512,512]{1,2,0:T(32,128)(4,1)S(1)}, pred[4,512,512]{1,2,0:T(32,128)(4,1)}, u32[]{:S(2)}) copy-start(pred[4,512,512]{1,2,0:T(32,128)(4,1)} %reshape.89) | copy-start | bytes 3145732
  51.7 11.1 %copy-start.16 = (f32[4,64]{1,0:T(4,128)S(1)}, f32[4,64]{1,0:T(4,128)}, u32[]{:S(2)}) copy-start(f32[4,64]{1,0:T(4,128)} %param.16) | copy-start | bytes 3076
  57.3 6.5 %copy-start.7 = (bf16[512,4,64]{0,2,1:T(8,128)(2,1)}, bf16[512,4,64]{0,2,1:T(8,128)(2,1)S(1)}, u32[]{:S(2)}) copy-start(bf16[512,4,64]{0,2,1:T(8,128)(2,1)S(1)} %squeeze.48) | copy-start | bytes 786436
  63.8 2.7 %copy-start.1 = (f32[4,512,512]{1,2,0:T(8,128)}, f32[4,512,512]{1,2,0:T(8,128)S(1)}, u32[]{:S(2)}) copy-start(f32[4,512,512]{1,2,0:T(8,128)S(1)} %fusion.1) | copy-start | bytes 12582916
  63.8 2.7 %copy-start.14 = (bf16[512,4,64]{0,2,1:T(8,128)(2,1)S(1)}, bf16[512,4,64]{0,2,1:T(8,128)(2,1)}, u32[]{:S(2)}) copy-start(bf16[512,4,64]{0,2,1:T(8,128)(2,1)} %squeeze.46) | copy-start | bytes 786436
  63.8 2.7 %copy-start.15 = (bf16[512,4,64]{0,2,1:T(8,128)(2,1)S(1)}, bf16[512,4,64]{0,2,1:T(8,128)(2,1)}, u32[]{:S(2)}) copy-start(bf16[512,4,64]{0,2,1:T(8,128)(2,1)} %squeeze.49) | copy-start | bytes 786436
  75.1 5.3 %copy-start.9 = (bf16[512,4,64]{0,2,1:T(8,128)(2,1)S(1)}, bf16[512,4,64]{0,2,1:T(8,128)(2,1)}, u32[]{:S(2)}) copy-start(bf16[512,4,64]{0,2,1:T(8,128)(2,1)} %squeeze.47) | copy-start | bytes 786436
  75.1 7.7 %copy-start.8 = (bf16[512,4,64]{0,2,1:T(8,128)(2,1)S(1)}, bf16[512,4,64]{0,2,1:T(8,128)(2,1)}, u32[]{:S(2)}) copy-start(bf16[512,4,64]{0,2,1:T(8,128)(2,1)} %copy-done.7) | copy-start | bytes 786436
  85.6 4.6 %copy-start.2 = (bf16[1,512,1024]{2,1,0:T(8,128)(2,1)S(1)}, bf16[1,512,1024]{2,1,0:T(8,128)(2,1)}, u32[]{:S(2)}) copy-start(bf16[1,512,1024]{2,1,0:T(8,128)(2,1)} %all-gather.5.cloned.1.call-done) | copy-start | bytes 3145732
  85.6 4.6 %copy-start.5 = (bf16[4,64,512]{2,1,0:T(8,128)(2,1)S(1)}, bf16[4,64,512]{2,1,0:T(8,128)(2,1)}, u32[]{:S(2)}) copy-start(bf16[4,64,512]{2,1,0:T(8,128)(2,1)} %fusion.2) | copy-start | bytes 786436
  97.3 4.5 %copy-start.6 = (bf16[4,64,512]{2,1,0:T(8,128)(2,1)S(1)}, bf16[4,64,512]{2,1,0:T(8,128)(2,1)}, u32[]{:S(2)}) copy-start(bf16[4,64,512]{2,1,0:T(8,128)(2,1)} %fusion.2) | copy-start | bytes 786436
  107.0 6.1 %copy-start.13 = (bf16[1,64,512]{2,1,0:T(8,128)(2,1)S(1)}, bf16[1,64,512]{2,1,0:T(8,128)(2,1)}, u32[]{:S(2)}) copy-start(bf16[1,64,512]{2,1,0:T(8,128)(2,1)} %param.15) | copy-start | bytes 196612
  107.0 27.0 %all-to-all-start = ((bf16[4,512,256]{2,0,1:T(4,128)(2,1)}), bf16[4,512,256]{2,0,1:T(4,128)(2,1)S(1)}, u32[]{:S(2)}, u32[]{:S(2)}) async-start(bf16[4,512,256]{2,0,1:T(4,128)(2,1)} %pad_maximum_fusion.2), calls=%async_computation | async-start | bytes 2097152 | tf_op jit(solution)/shard_map/all_to_all | solution.py:121
  110.7 63.3 %reduce-scatter.3.cloned.1.call-start = ((), (), s32[]{:S(2)}) async-start(), calls=%async_computation.3 | async-start | bytes 163840 | tf_op jit(solution)/shard_map/reduce_scatter | solution.py:136
  (2 other events, 2.7 us)
Sparse Core Ops, SparseCore 0:
  9.8 35.3 all-gather.4
  47.1 27.2 all-gather.6
  97.4 50.6 reduce-scatter.4
  151.3 22.6 reduce-scatter.2
